TPU v7x, 32 devices: a whole 2x2x4 slice. The times are simulated.
32 devices in a mesh: expert: 8 (over z, core), hid: 4 (over y, x).
Axes of the slice: x: 2, y: 2, z: 4, core: 2. Of those that a mesh axis runs over, the one named last changes fastest.
Arguments:
- tokens: bfloat16 [64, 3584], P('expert', 'hid'), may hold values from -6 to 6
- cotangent: bfloat16 [64, 3584], P('expert', 'hid'), may hold values from -6 to 6
- gate_prob: float32 [64, 8], P('expert'), may hold values from 0.1 to 1
- routes: int32 [64, 8], P('expert'), may hold values from 0 to 7, as said below
- slots: int32 [64, 8], P('expert'), may hold values from 0 to 8, as said below
- drop_seed: int32 [1], replicated, may hold values from 0 to 16777215
- layer_id: int32 [1], replicated, may hold values from 0 to 63
- w_gate: bfloat16 [8, 2560, 3584], P('expert', 'hid'), may hold values from -0.09375 to 0.09375
- w_up: bfloat16 [8, 2560, 3584], P('expert', 'hid'), may hold values from -0.09375 to 0.09375
- w_down: bfloat16 [8, 2560, 3584], P('expert', 'hid'), may hold values from -0.125 to 0.125
Outputs:
- grad_tokens: bfloat16 [64, 3584], P('expert', 'hid')
- grad_gate: bfloat16 [8, 2560, 3584], P('expert', 'hid')
- grad_up: bfloat16 [8, 2560, 3584], P('expert', 'hid')
- grad_down: bfloat16 [8, 2560, 3584], P('expert', 'hid')
Inputs may be any that keep to these rules, and one draw needn't show every extreme that they name: `routes`: each row names 8 different experts; one expert, drawn from the seed, is named by every token. Within one token group, the choices of each expert, taken in a priority order drawn from the seed, get slots 0, 1, 2 and so on, each slot at most once; those past 8 - 1 get the drop marker 8.
All inputs are finite; a program needn't handle non-finite values.
Results may differ from a plain program's by a relative error of at most 0.012.
Values may be sent and summed in bfloat16 or wider, within the bound.
No kernel may reach another device: no remote copies, remote signals or barrier semaphores. Data moves between devices by JAX's collectives and lax.ppermute only.
A program may use at most 64 MiB of HBM per device.

v0:
```python
import jax
import jax.numpy as jnp
from jax import lax
from jax.sharding import PartitionSpec as P

FF = 2560
CAP_SRC = 8
KEEP_FACTOR = 1024.0 / 922.0


def logical_shift(values, amount):
    return jnp.right_shift(values, amount) & (1 << 32 - amount) - 1


def keep_mask(counter, seed_value, layer_value):
    mixed = counter * -1640531535 + seed_value * 40503 + layer_value * 97
    mixed = mixed ^ logical_shift(mixed, 15)
    mixed = mixed * -2048144789
    mixed = mixed ^ logical_shift(mixed, 13)
    mixed = mixed * -1028477387
    mixed = mixed ^ logical_shift(mixed, 16)
    levels = logical_shift(mixed, 8) & 1023
    return jnp.where(levels >= 102, KEEP_FACTOR, 0.0).astype(jnp.float32)


def contract_rows(left, right):
    return lax.dot_general(
        left, right, (((0,), (0,)), ((), ())), preferred_element_type=jnp.float32
    )


def contract_cols(left, right):
    return lax.dot_general(
        left, right, (((1,), (1,)), ((), ())), preferred_element_type=jnp.float32
    )


def on_device(
    tokens, cotangent, gate_prob, routes, slots, drop_seed, layer_id, w_gate, w_up, w_down
):
    experts = lax.axis_size("expert")
    part_width = tokens.shape[1]
    capacity = experts * CAP_SRC
    local_units = w_gate.shape[1]
    target = jnp.where(slots < CAP_SRC, routes * CAP_SRC + slots, -1)
    slot_ids = jnp.arange(experts * CAP_SRC, dtype=jnp.int32)
    matches = target[None, :, :] == slot_ids[:, None, None]
    placed = jnp.any(matches, axis=2).astype(jnp.bfloat16)
    slot_gate = jnp.sum(jnp.where(matches, gate_prob[None, :, :], 0.0), axis=(1, 2))
    sent_x = jnp.dot(placed, tokens, preferred_element_type=jnp.float32).astype(jnp.bfloat16)
    plain_dy = jnp.dot(placed, cotangent, preferred_element_type=jnp.float32)
    sent_dy = (slot_gate[:, None] * plain_dy).astype(jnp.bfloat16)
    send_shape = (experts, CAP_SRC * part_width)
    recv_x, recv_dy = (
        lax.all_to_all(
            sent_x.reshape(send_shape), "expert", split_axis=0, concat_axis=0, tiled=True
        ),
        lax.all_to_all(
            sent_dy.reshape(send_shape), "expert", split_axis=0, concat_axis=0, tiled=True
        ),
    )
    rows_x, rows_dy = (
        lax.all_gather(recv_x.reshape(capacity, part_width), "hid", axis=1, tiled=True),
        lax.all_gather(recv_dy.reshape(capacity, part_width), "hid", axis=1, tiled=True),
    )
    gate_w = w_gate[0]
    up_w = w_up[0]
    down_w = w_down[0]
    gate_pre = contract_cols(rows_x, gate_w)
    up_pre = contract_cols(rows_x, up_w)
    expert_id = lax.axis_index("expert")
    unit_ids = lax.axis_index("hid") * local_units + jnp.arange(local_units, dtype=jnp.int32)
    row_ids = jnp.arange(capacity, dtype=jnp.int32)
    counter = (expert_id * capacity + row_ids[:, None]) * FF + unit_ids[None, :]
    keep_mul = keep_mask(counter, drop_seed[0], layer_id[0])
    logistic = jax.nn.sigmoid(gate_pre)
    swish = gate_pre * logistic
    hidden = (swish * up_pre * keep_mul).astype(jnp.bfloat16)
    grad_hidden = contract_cols(rows_dy, down_w) * keep_mul
    grad_upre = (grad_hidden * swish).astype(jnp.bfloat16)
    grad_gpre = (grad_hidden * up_pre * logistic * (1.0 + gate_pre * (1.0 - logistic))).astype(
        jnp.bfloat16
    )
    grad_down = contract_rows(hidden, rows_dy).astype(jnp.bfloat16)
    grad_gate = contract_rows(grad_gpre, rows_x).astype(jnp.bfloat16)
    grad_up = contract_rows(grad_upre, rows_x).astype(jnp.bfloat16)
    partial_sum = jnp.dot(grad_gpre, gate_w, preferred_element_type=jnp.float32) + jnp.dot(
        grad_upre, up_w, preferred_element_type=jnp.float32
    )
    summed = lax.psum(partial_sum.astype(jnp.bfloat16), "hid").astype(jnp.float32)
    own_cols = lax.dynamic_slice_in_dim(summed, lax.axis_index("hid") * part_width, part_width, 1)
    back_rows = lax.all_to_all(
        own_cols.astype(jnp.bfloat16).reshape(send_shape),
        "expert",
        split_axis=0,
        concat_axis=0,
        tiled=True,
    )
    grad_tokens = contract_rows(placed, back_rows.reshape(experts * CAP_SRC, part_width)).astype(
        jnp.bfloat16
    )
    return (grad_tokens, grad_gate[None], grad_up[None], grad_down[None])


def solution(mesh):
    in_specs = (
        P("expert", "hid"),
        P("expert", "hid"),
        P("expert", None),
        P("expert", None),
        P("expert", None),
        P(),
        P(),
        P("expert", "hid", None),
        P("expert", "hid", None),
        P("expert", "hid", None),
    )
    out_specs = (
        P("expert", "hid"),
        P("expert", "hid", None),
        P("expert", "hid", None),
        P("expert", "hid", None),
    )
    return jax.shard_map(
        on_device, mesh=mesh, in_specs=in_specs, out_specs=out_specs, check_vma=False
    )
```

profile of v0, /device:TPU:1, one launch (start us, length us, event | category | flops | bytes accessed | tf_op | source)
XLA Modules:
  0.0 131.4 jit_solution(13579242598336714023)
XLA Ops:
  7.2 0.0 copy-start
  7.2 0.7 add_select_fusion
  7.9 0.1 fusion.22
  8.0 0.8 select_reduce_fusion
  8.8 0.0 copy-done
  8.8 0.2 fusion.13
  9.1 0.5 broadcast.36
  9.6 1.3 reduce.4
  10.9 0.7 reshape.58
  11.6 6.4 %all-to-all-start = ((bf16[8,2,3584]{2,1,0:T(2,128)(2,1)}), bf16[8,2,3584]{2,1,0:T(2,128)(2,1)S(1)}, u32[]{:S(2)}, u32[]{:S(2)}) async-start(bf16[8,2,3584]{2,1,0:T(2,128)(2,1)} %reshape.58), calls=%async_computation | async-start | bytes 229376 | tf_op jit(solution)/shard_map/all_to_all | solution.py:58
  19.3 0.9 convolution_convert_fusion.3
  20.3 1.3 %reduce.3 = bf16[8,7168]{1,0:T(8,128)(2,1)S(1)} reduce(bf16[8,1,7168]{2,1,0:T(2,128)(2,1)S(1)} %all_to_all.25, bf16[]{:T(256)} %broadcast.36), dimensions={1}, to_apply=%all_to_all.25.reduce_sub_computation | reduce | bytes 229378 | tf_op jit(solution)/shard_map/all_to_all | solution.py:55
  21.6 0.7 reshape.56
  22.3 1.4 %all-to-all-done = bf16[8,2,3584]{2,1,0:T(2,128)(2,1)S(1)} async-done(((bf16[8,2,3584]{2,1,0:T(2,128)(2,1)}), bf16[8,2,3584]{2,1,0:T(2,128)(2,1)S(1)}, u32[]{:S(2)}, u32[]{:S(2)}) %all-to-all-start) | async-done | bytes 114720 | tf_op jit(solution)/shard_map/all_to_all | solution.py:58
  23.7 4.1 %all-to-all-start.1 = ((bf16[8,2,3584]{2,1,0:T(2,128)(2,1)}), bf16[8,2,3584]{2,1,0:T(2,128)(2,1)S(1)}, u32[]{:S(2)}, u32[]{:S(2)}) async-start(bf16[8,2,3584]{2,1,0:T(2,128)(2,1)} %reshape.56), calls=%async_computation.1 | async-start | bytes 229376 | tf_op jit(solution)/shard_map/all_to_all | solution.py:55
  27.8 0.0 all-reduce.2.cloned.1.call-start
  27.8 0.1 reshape.59
  27.9 0.7 reduce
  28.6 0.1 reshape.50
  28.7 4.9 %all-to-all-done.1 = bf16[8,2,3584]{2,1,0:T(2,128)(2,1)S(1)} async-done(((bf16[8,2,3584]{2,1,0:T(2,128)(2,1)}), bf16[8,2,3584]{2,1,0:T(2,128)(2,1)S(1)}, u32[]{:S(2)}, u32[]{:S(2)}) %all-to-all-start.1) | async-done | bytes 114720 | tf_op jit(solution)/shard_map/all_to_all | solution.py:55
  33.5 0.1 reshape.57
  33.6 0.7 reduce.1
  34.3 0.1 reshape.51
  34.4 0.0 copy-start.1
  34.4 0.0 copy-start.2
  34.4 8.3 %all_gather.7 = bf16[64,3584]{1,0:T(8,128)(2,1)S(1)} all-gather(bf16[64,896]{1,0:T(8,128)(2,1)S(1)} %reshape.51), channel_id=1, replica_groups=mesh['expert'=8,'hid'=4] {'hid'}, dimensions={1}, use_global_device_ids=true | all-gather | bytes 573440 | tf_op jit(solution)/shard_map/all_gather | solution.py:63
  42.7 0.0 slice-start
  42.7 4.0 %fusion.6 = f32[64,640]{1,0:T(8,128)S(1)} fusion(bf16[64,3584]{1,0:T(8,128)(2,1)S(1)} %all_gather.7, bf16[1,640,3584]{2,1,0:T(8,128)(2,1)} %param.17), kind=kOutput, calls=%fused_computation.10 | convolution fusion | flops 293601280 | bytes 5210112 | tf_op jit(solution)/shard_map/dot_general | solution.py:33
  46.7 0.0 copy-done.1
  46.7 0.0 slice-start.1
  46.7 1.5 %fusion.9 = f32[64,640]{1,0:T(8,128)S(1)} fusion(bf16[64,3584]{1,0:T(8,128)(2,1)S(1)} %all_gather.7, bf16[1,640,3584]{2,1,0:T(8,128)(2,1)S(1)} %copy-done.1), kind=kOutput, calls=%fused_computation.13 | convolution fusion | flops 293601280 | bytes 5210112 | tf_op jit(solution)/shard_map/dot_general | solution.py:33
  48.2 8.6 %all_gather.6 = bf16[64,3584]{1,0:T(8,128)(2,1)S(1)} all-gather(bf16[64,896]{1,0:T(8,128)(2,1)S(1)} %reshape.50), channel_id=1, replica_groups=mesh['expert'=8,'hid'=4] {'hid'}, dimensions={1}, use_global_device_ids=true | all-gather | bytes 573440 | tf_op jit(solution)/shard_map/all_gather | solution.py:64
  56.8 0.0 copy-done.2
  56.8 1.5 %multiply_convert_fusion = (bf16[64,640]{1,0:T(8,128)(2,1)S(1)}, bf16[64,640]{1,0:T(8,128)(2,1)S(1)}) fusion(f32[64,640]{1,0:T(8,128)S(1)} %fusion.6, f32[64,640]{1,0:T(8,128)S(1)} %fusion.9, s32[]{:T(128)} %bitcast.2, s32[]{:T(128)} %bitcast.1, s32[640]{0:T(1024)S(1)} %iota_add_fusion, s32[64]{0:T(128)S(1)} %add_multiply_fusion, ...), kind=kOutput, calls=%fused_computation.25 | convolution fusion | flops 294993920 | bytes 5540616 | tf_op jit(solution)/shard_map/dot_general | solution.py:33
  58.4 0.0 slice-done
  58.4 0.0 slice-done.1
  58.4 0.9 fusion.4
  59.3 1.7 %fusion.3 = bf16[64,3584]{1,0:T(8,128)(2,1)} fusion(f32[64,3584]{1,0:T(8,128)S(1)} %fusion.4, bf16[64,640]{1,0:T(8,128)(2,1)S(1)} %get-tuple-element.4, bf16[1,640,3584]{2,1,0:T(8,128)(2,1)S(1)} %copy-done.1), kind=kOutput, calls=%fused_computation.7 | convolution fusion | flops 294060032 | bytes 6045696 | tf_op jit(solution)/shard_map/dot_general | solution.py:87
  61.0 0.0 all-reduce.2.cloned.1.call-update
  61.0 3.5 %fusion.1 = bf16[1,640,3584]{2,1,0:T(8,128)(2,1)} fusion(bf16[64,640]{1,0:T(8,128)(2,1)S(1)} %get-tuple-element.4, bf16[64,3584]{1,0:T(8,128)(2,1)S(1)} %all_gather.7), kind=kOutput, calls=%fused_computation.4 | convolution fusion | flops 295895040 | bytes 5128192 | tf_op jit(solution)/shard_map/dot_general | solution.py:27
  64.6 42.6 %all-reduce.2.cloned.1.call-done = bf16[64,3584]{1,0:T(8,128)(2,1)} async-done(((bf16[64,3584]{1,0:T(8,128)(2,1)}), bf16[64,3584]{1,0:T(8,128)(2,1)}) %all-reduce.2.cloned.1.call-update) | async-done | bytes 458768 | tf_op jit(solution)/shard_map/psum | solution.py:90
  107.1 0.9 convert_convert_fusion
  108.1 1.3 %reduce.5 = bf16[8,7168]{1,0:T(8,128)(2,1)S(1)} reduce(bf16[8,1,7168]{2,1,0:T(2,128)(2,1)S(1)} %all_to_all.26, bf16[]{:T(256)} %broadcast.36), dimensions={1}, to_apply=%all_to_all.26.reduce_sub_computation | reduce | bytes 229378 | tf_op jit(solution)/shard_map/all_to_all | solution.py:92
  109.4 0.7 reshape.60
  110.1 5.7 %all-to-all-start.2 = ((bf16[8,2,3584]{2,1,0:T(2,128)(2,1)}), bf16[8,2,3584]{2,1,0:T(2,128)(2,1)S(1)}, u32[]{:S(2)}, u32[]{:S(2)}) async-start(bf16[8,2,3584]{2,1,0:T(2,128)(2,1)} %reshape.60), calls=%async_computation.2 | async-start | bytes 229376 | tf_op jit(solution)/shard_map/all_to_all | solution.py:92
  115.8 3.5 %fusion = bf16[1,640,3584]{2,1,0:T(8,128)(2,1)} fusion(bf16[64,640]{1,0:T(8,128)(2,1)S(1)} %get-tuple-element.5, bf16[64,3584]{1,0:T(8,128)(2,1)S(1)} %all_gather.7), kind=kOutput, calls=%fused_computation.3 | convolution fusion | flops 295895040 | bytes 5128192 | tf_op jit(solution)/shard_map/dot_general | solution.py:27
  119.3 3.6 %fusion.2 = bf16[1,640,3584]{2,1,0:T(8,128)(2,1)} fusion(bf16[64,3584]{1,0:T(8,128)(2,1)S(1)} %all_gather.6, f32[64,640]{1,0:T(8,128)S(1)} %fusion.9, s32[]{:T(128)} %bitcast.2, s32[]{:T(128)} %bitcast.1, s32[640]{0:T(1024)S(1)} %iota_add_fusion, s32[64]{0:T(128)S(1)} %add_multiply_fusion, f32[64,640]{1,0:T(8,128)S(1)} %fusion.6), kind=kOutput, calls=%fused_computation.5 | convolution fusion | flops 297000960 | bytes 5376776 | tf_op jit(solution)/shard_map/dot_general | solution.py:27
  123.0 0.0 all-to-all-done.2
  123.0 0.1 reshape.61
  123.1 0.6 reduce.2
  123.7 0.1 reshape.52
  123.8 0.7 convolution_convert_fusion.4
  (6 shorter events, 0.1 us)
Async XLA Ops:
  7.2 1.6 %copy-start = (bf16[8,896]{1,0:T(8,128)(2,1)S(1)}, bf16[8,896]{1,0:T(8,128)(2,1)}, u32[]{:S(2)}) copy-start(bf16[8,896]{1,0:T(8,128)(2,1)} %param.11) | copy-start | bytes 43012
  11.6 12.1 %all-to-all-start = ((bf16[8,2,3584]{2,1,0:T(2,128)(2,1)}), bf16[8,2,3584]{2,1,0:T(2,128)(2,1)S(1)}, u32[]{:S(2)}, u32[]{:S(2)}) async-start(bf16[8,2,3584]{2,1,0:T(2,128)(2,1)} %reshape.58), calls=%async_computation | async-start | bytes 229376 | tf_op jit(solution)/shard_map/all_to_all | solution.py:58
  23.7 9.9 %all-to-all-start.1 = ((bf16[8,2,3584]{2,1,0:T(2,128)(2,1)}), bf16[8,2,3584]{2,1,0:T(2,128)(2,1)S(1)}, u32[]{:S(2)}, u32[]{:S(2)}) async-start(bf16[8,2,3584]{2,1,0:T(2,128)(2,1)} %reshape.56), calls=%async_computation.1 | async-start | bytes 229376 | tf_op jit(solution)/shard_map/all_to_all | solution.py:55
  27.8 79.3 %all-reduce.2.cloned.1.call-start = ((), (), s32[]{:S(2)}) async-start(), calls=%async_computation.3 | async-start | bytes 917504 | tf_op jit(solution)/shard_map/psum | solution.py:90
  34.4 12.3 %copy-start.1 = (bf16[1,640,3584]{2,1,0:T(8,128)(2,1)S(1)}, bf16[1,640,3584]{2,1,0:T(8,128)(2,1)}, u32[]{:S(2)}) copy-start(bf16[1,640,3584]{2,1,0:T(8,128)(2,1)} %param.18) | copy-start | bytes 13762564
  34.4 22.5 %copy-start.2 = (bf16[1,640,3584]{2,1,0:T(8,128)(2,1)S(1)}, bf16[1,640,3584]{2,1,0:T(8,128)(2,1)}, u32[]{:S(2)}) copy-start(bf16[1,640,3584]{2,1,0:T(8,128)(2,1)} %param.19) | copy-start | bytes 13762564
  42.7 15.7 %slice-start = ((s8[4587520]{0:T(1024)(128)(4,1)}), s8[4194304]{0:T(1024)(128)(4,1)S(1)}, s32[]{:S(2)}) async-start(s8[4587520]{0:T(1024)(128)(4,1)} %bitcast.41), calls=%async_computation.4 | async-start | bytes 8388608
  46.7 11.7 %slice-start.1 = ((s8[4587520]{0:T(1024)(128)(4,1)}), s8[393216]{0:T(1024)(128)(4,1)S(1)}, s32[]{:S(2)}) async-start(s8[4587520]{0:T(1024)(128)(4,1)} %bitcast.41), calls=%async_computation.5 | async-start | bytes 786432
  110.1 12.9 %all-to-all-start.2 = ((bf16[8,2,3584]{2,1,0:T(2,128)(2,1)}), bf16[8,2,3584]{2,1,0:T(2,128)(2,1)S(1)}, u32[]{:S(2)}, u32[]{:S(2)}) async-start(bf16[8,2,3584]{2,1,0:T(2,128)(2,1)} %reshape.60), calls=%async_computation.2 | async-start | bytes 229376 | tf_op jit(solution)/shard_map/all_to_all | solution.py:92
Sparse Core Ops, SparseCore 0:
  61.2 45.9 all-reduce.1
where the time goes:
time: 132 us; the launch traced here: 131 us
  waiting for transfers between devices  48.8 us (37%)
  matrix products  22.2 us (17%)
  blocking collectives  16.9 us (13%)
  starting transfers between devices  16.2 us (12%)
  between operations  15.5 us (12%)
  other arithmetic  8.46 us (6%)
  local copies, waits for them, and re-layouts  3.23 us (2%)
    psum x1, waiting for transfers between devices, on_device(): lax.psum(partial_sum.astype(jnp.bfloat16), 'hid').astype(jnp.float32)  42.6 us
    dot_general x4, matrix products, contract_rows(): lax.dot_general(left, right, (((0,), (0,)), ((), ())), preferred_element_...  11.4 us
    all_gather x1, blocking collectives, on_device(): lax.all_gather(recv_dy.reshape(capacity, part_width), 'hid', axis=1, tile...  8.65 us
    all_gather x1, blocking collectives, on_device(): lax.all_gather(recv_x.reshape(capacity, part_width), 'hid', axis=1, tiled...  8.3 us
    dot_general x3, matrix products, contract_cols(): lax.dot_general(left, right, (((1,), (1,)), ((), ())), preferred_element_...  6.98 us
    all_to_all x1, starting transfers between devices, on_device(): lax.all_to_all(sent_dy.reshape(send_shape), 'expert', split_axis=0, conca...  6.38 us
    all_to_all x1, starting transfers between devices, on_device(): lax.all_to_all(own_cols.astype(jnp.bfloat16).reshape(send_shape), 'expert...  5.71 us
    all_to_all x1, waiting for transfers between devices, on_device(): lax.all_to_all(sent_x.reshape(send_shape), 'expert', split_axis=0, concat...  4.86 us
  transfers between devices with their start and end apart: 4, of which 3 were waited for; matrix products, arithmetic and copies ran while one was open for 11% of the time, Pallas kernels for 0%

commit v1 on v0

--- a/solution.py
+++ b/solution.py
@@ -59,8 +59,22 @@
             sent_dy.reshape(send_shape), "expert", split_axis=0, concat_axis=0, tiled=True
         ),
     )
+
+    def halves_proceed(sheet, named_axis):
+        y1, built = (lax.axis_size(named_axis), lax.axis_index(named_axis))
+        current_value, z = (sheet, 1)
+        while z < y1:
+            local_part = lax.ppermute(
+                current_value, axis_name=named_axis, perm=tuple(((it, it ^ z) for it in range(y1)))
+            )
+            work_now = jnp.concatenate([current_value, local_part], axis=1)
+            z1 = jnp.concatenate([local_part, current_value], axis=1)
+            current_value = jnp.where(built & z == 0, work_now, z1)
+            z = 2 * z
+        return current_value
+
     rows_x, rows_dy = (
-        lax.all_gather(recv_x.reshape(capacity, part_width), "hid", axis=1, tiled=True),
+        halves_proceed(recv_x.reshape(capacity, part_width), "hid"),
         lax.all_gather(recv_dy.reshape(capacity, part_width), "hid", axis=1, tiled=True),
     )
     gate_w = w_gate[0]

time: 132 us -> 127 us (0.962)
  blocking collectives: 16.9 us -> 8.3 us
  starting transfers between devices: 16.2 us -> 19.1 us
    all_gather x1 -> x0, blocking collectives: 8.3 us -> none  [on_device(): lax.all_gather(recv_x.reshape(capacity, part_width), 'hid', axis=1, tiled...]
    ppermute x0 -> x2, starting transfers between devices: none -> 2.58 us  [halves_proceed(): lax.ppermute(current_value, axis_name=named_axis, perm=tuple(((it, it ^ z...]
    all_to_all x1, starting transfers between devices: 4.14 us -> 6.38 us  [on_device(): lax.all_to_all(sent_x.reshape(send_shape), 'expert', split_axis=0, concat...]
    all_to_all x1, starting transfers between devices: 6.38 us -> 4.42 us  [on_device(): lax.all_to_all(sent_dy.reshape(send_shape), 'expert', split_axis=0, conca...]
    all_to_all x1, waiting for transfers between devices: 1.36 us -> 3.03 us  [on_device(): lax.all_to_all(sent_dy.reshape(send_shape), 'expert', split_axis=0, conca...]
    psum x1, waiting for transfers between devices: 42.6 us -> 41.2 us  [on_device(): lax.psum(partial_sum.astype(jnp.bfloat16), 'hid').astype(jnp.float32)]
  transfers between devices with their start and end apart: 4 -> 6, of which waited for: 3 -> 3; matrix products, arithmetic and copies ran while one was open for 11% -> 12% of each run, Pallas kernels for 0% -> 0%
where the time goes in v1:
time: 127 us; the launch traced here: 126 us
  waiting for transfers between devices  49.1 us (39%)
  matrix products  22.2 us (17%)
  starting transfers between devices  19.1 us (15%)
  between operations  15.5 us (12%)
  other arithmetic  8.52 us (7%)
  blocking collectives  8.3 us (7%)
  local copies, waits for them, and re-layouts  3.23 us (3%)
    psum x1, waiting for transfers between devices, on_device(): lax.psum(partial_sum.astype(jnp.bfloat16), 'hid').astype(jnp.float32)  41.2 us
    dot_general x4, matrix products, contract_rows(): lax.dot_general(left, right, (((0,), (0,)), ((), ())), preferred_element_...  11.4 us
    all_gather x1, blocking collectives, on_device(): lax.all_gather(recv_dy.reshape(capacity, part_width), 'hid', axis=1, tile...  8.3 us
    dot_general x3, matrix products, contract_cols(): lax.dot_general(left, right, (((1,), (1,)), ((), ())), preferred_element_...  6.97 us
    all_to_all x1, starting transfers between devices, on_device(): lax.all_to_all(sent_x.reshape(send_shape), 'expert', split_axis=0, concat...  6.38 us
    all_to_all x1, starting transfers between devices, on_device(): lax.all_to_all(own_cols.astype(jnp.bfloat16).reshape(send_shape), 'expert...  5.71 us
    all_to_all x1, waiting for transfers between devices, on_device(): lax.all_to_all(sent_x.reshape(send_shape), 'expert', split_axis=0, concat...  4.91 us
    all_to_all x1, starting transfers between devices, on_device(): lax.all_to_all(sent_dy.reshape(send_shape), 'expert', split_axis=0, conca...  4.42 us
  transfers between devices with their start and end apart: 6, of which 3 were waited for; matrix products, arithmetic and copies ran while one was open for 12% of the time, Pallas kernels for 0%

profile of v1, /device:TPU:1, one launch (start us, length us, event | category | flops | bytes accessed | tf_op | source)
XLA Modules:
  0.0 126.0 jit_solution(16257892778137474524)
XLA Ops:
  7.2 0.0 copy-start
  7.2 0.7 add_select_fusion
  7.9 0.1 fusion.22
  8.0 0.0 copy-done
  8.0 0.2 convolution_convert_fusion.3
  8.3 0.5 broadcast.36
  8.8 1.3 %reduce.3 = bf16[8,7168]{1,0:T(8,128)(2,1)S(1)} reduce(bf16[8,1,7168]{2,1,0:T(2,128)(2,1)S(1)} %all_to_all.25, bf16[]{:T(256)} %broadcast.36), dimensions={1}, to_apply=%all_to_all.25.reduce_sub_computation | reduce | bytes 229378 | tf_op jit(solution)/shard_map/all_to_all | solution.py:55
  10.1 0.7 reshape.56
  10.8 6.4 %all-to-all-start.1 = ((bf16[8,2,3584]{2,1,0:T(2,128)(2,1)}), bf16[8,2,3584]{2,1,0:T(2,128)(2,1)S(1)}, u32[]{:S(2)}, u32[]{:S(2)}) async-start(bf16[8,2,3584]{2,1,0:T(2,128)(2,1)} %reshape.56), calls=%async_computation.1 | async-start | bytes 229376 | tf_op jit(solution)/shard_map/all_to_all | solution.py:55
  17.2 0.8 select_reduce_fusion
  18.0 4.9 %all-to-all-done.1 = bf16[8,2,3584]{2,1,0:T(2,128)(2,1)S(1)} async-done(((bf16[8,2,3584]{2,1,0:T(2,128)(2,1)}), bf16[8,2,3584]{2,1,0:T(2,128)(2,1)S(1)}, u32[]{:S(2)}, u32[]{:S(2)}) %all-to-all-start.1) | async-done | bytes 114720 | tf_op jit(solution)/shard_map/all_to_all | solution.py:55
  22.9 0.1 reshape.57
  23.0 0.7 reduce.1
  23.7 0.1 reshape.51
  23.7 1.3 %collective-permute-start = (bf16[64,896]{1,0:T(8,128)(2,1)S(1)}, bf16[64,896]{1,0:T(8,128)(2,1)S(1)}, u32[]{:S(2)}, u32[]{:S(2)}) collective-permute-start(bf16[64,896]{1,0:T(8,128)(2,1)S(1)} %reshape.51), channel_id=1, source_target_pairs={{0,1},{1,0},{2,3},{3,2},{4,5},{5,4},{6,7},{7,6},{8,9},{9,8},{10,11... | collective-permute-start | bytes 344072 | tf_op jit(solution)/shard_map/ppermute | solution.py:67
  25.0 0.9 fusion.13
  26.0 1.3 %reduce.4 = bf16[8,7168]{1,0:T(8,128)(2,1)S(1)} reduce(bf16[8,1,7168]{2,1,0:T(2,128)(2,1)S(1)} %all_to_all.24, bf16[]{:T(256)} %broadcast.36), dimensions={1}, to_apply=%all_to_all.24.reduce_sub_computation | reduce | bytes 229378 | tf_op jit(solution)/shard_map/all_to_all | solution.py:58
  27.3 0.7 reshape.58
  28.0 4.4 %all-to-all-start = ((bf16[8,2,3584]{2,1,0:T(2,128)(2,1)}), bf16[8,2,3584]{2,1,0:T(2,128)(2,1)S(1)}, u32[]{:S(2)}, u32[]{:S(2)}) async-start(bf16[8,2,3584]{2,1,0:T(2,128)(2,1)} %reshape.58), calls=%async_computation | async-start | bytes 229376 | tf_op jit(solution)/shard_map/all_to_all | solution.py:58
  32.4 0.0 all-reduce.2.cloned.1.call-start
  32.5 0.0 collective-permute-done
  32.5 0.1 maximum_select_fusion.1
  32.5 1.3 %collective-permute-start.1 = (bf16[64,1792]{1,0:T(8,128)(2,1)S(1)}, bf16[64,1792]{1,0:T(8,128)(2,1)S(1)}, u32[]{:S(2)}, u32[]{:S(2)}) collective-permute-start(bf16[64,1792]{1,0:T(8,128)(2,1)S(1)} %maximum_select_fusion.1), channel_id=1, source_target_pairs={{0,2},{1,3},{2,0},{3,1},{4,6},{5,7},{6,4},{7,5},{8,10},{9,11},{10,... | collective-permute-start | bytes 688136 | tf_op jit(solution)/shard_map/ppermute | solution.py:67
  35.1 3.0 %all-to-all-done = bf16[8,2,3584]{2,1,0:T(2,128)(2,1)S(1)} async-done(((bf16[8,2,3584]{2,1,0:T(2,128)(2,1)}), bf16[8,2,3584]{2,1,0:T(2,128)(2,1)S(1)}, u32[]{:S(2)}, u32[]{:S(2)}) %all-to-all-start) | async-done | bytes 114720 | tf_op jit(solution)/shard_map/all_to_all | solution.py:58
  38.2 0.1 reshape.59
  38.3 0.7 reduce
  39.0 0.1 reshape.50
  39.0 0.0 copy-start.1
  39.0 8.3 %all_gather.3 = bf16[64,3584]{1,0:T(8,128)(2,1)S(1)} all-gather(bf16[64,896]{1,0:T(8,128)(2,1)S(1)} %reshape.50), channel_id=1, replica_groups=mesh['expert'=8,'hid'=4] {'hid'}, dimensions={1}, use_global_device_ids=true | all-gather | bytes 573440 | tf_op jit(solution)/shard_map/all_gather | solution.py:78
  47.3 0.0 copy-start.2
  47.3 0.0 collective-permute-done.1
  47.3 0.0 slice-start
  47.3 3.9 %fusion.6 = f32[64,640]{1,0:T(8,128)S(1)} fusion(bf16[1,640,3584]{2,1,0:T(8,128)(2,1)} %param.17, bf16[64,1792]{1,0:T(8,128)(2,1)S(1)} %collective-permute-done.1, bf16[64,1792]{1,0:T(8,128)(2,1)S(1)} %maximum_select_fusion.1, pred[]{:T(512)S(6)} %eq.22), kind=kOutput, calls=%fused_computation.10 | convolution fusion | flops 295665664 | bytes 5210113 | tf_op jit(solution)/shard_map/dot_general | solution.py:33
  51.3 0.0 copy-done.1
  51.3 0.0 slice-start.1
  51.3 1.5 %fusion.9 = f32[64,640]{1,0:T(8,128)S(1)} fusion(bf16[1,640,3584]{2,1,0:T(8,128)(2,1)S(1)} %copy-done.1, bf16[64,1792]{1,0:T(8,128)(2,1)S(1)} %collective-permute-done.1, bf16[64,1792]{1,0:T(8,128)(2,1)S(1)} %maximum_select_fusion.1, pred[]{:T(512)S(6)} %eq.22), kind=kOutput, calls=%fused_computation.13 | convolution fusion | flops 295665664 | bytes 5210113 | tf_op jit(solution)/shard_map/dot_general | solution.py:33
  52.8 0.0 copy-done.2
  52.9 1.5 %multiply_convert_fusion = (bf16[64,640]{1,0:T(8,128)(2,1)S(1)}, bf16[64,640]{1,0:T(8,128)(2,1)S(1)}) fusion(f32[64,640]{1,0:T(8,128)S(1)} %fusion.6, f32[64,640]{1,0:T(8,128)S(1)} %fusion.9, s32[]{:T(128)} %bitcast.2, s32[]{:T(128)} %bitcast.1, s32[640]{0:T(1024)S(1)} %iota_add_fusion, s32[64]{0:T(128)S(1)} %add_multiply_fusion, ...), kind=kOutput, calls=%fused_computation.27 | convolution fusion | flops 294993920 | bytes 5540616 | tf_op jit(solution)/shard_map/dot_general | solution.py:33
  54.4 0.0 slice-done
  54.4 0.0 slice-done.1
  54.4 0.9 fusion.4
  55.3 1.7 %fusion.3 = bf16[64,3584]{1,0:T(8,128)(2,1)} fusion(f32[64,3584]{1,0:T(8,128)S(1)} %fusion.4, bf16[64,640]{1,0:T(8,128)(2,1)S(1)} %get-tuple-element.4, bf16[1,640,3584]{2,1,0:T(8,128)(2,1)S(1)} %copy-done.1), kind=kOutput, calls=%fused_computation.7 | convolution fusion | flops 294060032 | bytes 6045696 | tf_op jit(solution)/shard_map/dot_general | solution.py:101
  57.0 0.0 all-reduce.2.cloned.1.call-update
  57.1 3.5 %fusion.1 = bf16[1,640,3584]{2,1,0:T(8,128)(2,1)} fusion(bf16[64,640]{1,0:T(8,128)(2,1)S(1)} %get-tuple-element.4, bf16[64,1792]{1,0:T(8,128)(2,1)S(1)} %collective-permute-done.1, bf16[64,1792]{1,0:T(8,128)(2,1)S(1)} %maximum_select_fusion.1, pred[]{:T(512)S(6)} %eq.22), kind=kOutput, calls=%fused_computation.4 | convolution fusion | flops 297959424 | bytes 5128193 | tf_op jit(solution)/shard_map/dot_general | solution.py:27
  60.6 41.2 %all-reduce.2.cloned.1.call-done = bf16[64,3584]{1,0:T(8,128)(2,1)} async-done(((bf16[64,3584]{1,0:T(8,128)(2,1)}), bf16[64,3584]{1,0:T(8,128)(2,1)}) %all-reduce.2.cloned.1.call-update) | async-done | bytes 458768 | tf_op jit(solution)/shard_map/psum | solution.py:104
  101.8 0.9 convert_convert_fusion
  102.7 1.3 %reduce.5 = bf16[8,7168]{1,0:T(8,128)(2,1)S(1)} reduce(bf16[8,1,7168]{2,1,0:T(2,128)(2,1)S(1)} %all_to_all.26, bf16[]{:T(256)} %broadcast.36), dimensions={1}, to_apply=%all_to_all.26.reduce_sub_computation | reduce | bytes 229378 | tf_op jit(solution)/shard_map/all_to_all | solution.py:106
  104.0 0.7 reshape.60
  104.7 5.7 %all-to-all-start.2 = ((bf16[8,2,3584]{2,1,0:T(2,128)(2,1)}), bf16[8,2,3584]{2,1,0:T(2,128)(2,1)S(1)}, u32[]{:S(2)}, u32[]{:S(2)}) async-start(bf16[8,2,3584]{2,1,0:T(2,128)(2,1)} %reshape.60), calls=%async_computation.2 | async-start | bytes 229376 | tf_op jit(solution)/shard_map/all_to_all | solution.py:106
  110.5 3.5 %fusion = bf16[1,640,3584]{2,1,0:T(8,128)(2,1)} fusion(bf16[64,640]{1,0:T(8,128)(2,1)S(1)} %get-tuple-element.5, bf16[64,1792]{1,0:T(8,128)(2,1)S(1)} %collective-permute-done.1, bf16[64,1792]{1,0:T(8,128)(2,1)S(1)} %maximum_select_fusion.1, pred[]{:T(512)S(6)} %eq.22), kind=kOutput, calls=%fused_computation.3 | convolution fusion | flops 297959424 | bytes 5128193 | tf_op jit(solution)/shard_map/dot_general | solution.py:27
  114.0 3.6 %fusion.2 = bf16[1,640,3584]{2,1,0:T(8,128)(2,1)} fusion(bf16[64,3584]{1,0:T(8,128)(2,1)S(1)} %all_gather.3, f32[64,640]{1,0:T(8,128)S(1)} %fusion.9, s32[]{:T(128)} %bitcast.2, s32[]{:T(128)} %bitcast.1, s32[640]{0:T(1024)S(1)} %iota_add_fusion, s32[64]{0:T(128)S(1)} %add_multiply_fusion, f32[64,640]{1,0:T(8,128)S(1)} %fusion.6), kind=kOutput, calls=%fused_computation.5 | convolution fusion | flops 297000960 | bytes 5376776 | tf_op jit(solution)/shard_map/dot_general | solution.py:27
  117.6 0.0 all-to-all-done.2
  117.6 0.1 reshape.61
  117.7 0.6 reduce.2
  118.4 0.1 reshape.52
  118.4 0.7 convolution_convert_fusion.4
  (6 shorter events, 0.1 us)
Async XLA Ops:
  7.2 0.8 copy-start
  10.8 12.1 %all-to-all-start.1 = ((bf16[8,2,3584]{2,1,0:T(2,128)(2,1)}), bf16[8,2,3584]{2,1,0:T(2,128)(2,1)S(1)}, u32[]{:S(2)}, u32[]{:S(2)}) async-start(bf16[8,2,3584]{2,1,0:T(2,128)(2,1)} %reshape.56), calls=%async_computation.1 | async-start | bytes 229376 | tf_op jit(solution)/shard_map/all_to_all | solution.py:55
  23.7 8.7 %collective-permute-start = (bf16[64,896]{1,0:T(8,128)(2,1)S(1)}, bf16[64,896]{1,0:T(8,128)(2,1)S(1)}, u32[]{:S(2)}, u32[]{:S(2)}) collective-permute-start(bf16[64,896]{1,0:T(8,128)(2,1)S(1)} %reshape.51), channel_id=1, source_target_pairs={{0,1},{1,0},{2,3},{3,2},{4,5},{5,4},{6,7},{7,6},{8,9},{9,8},{10,11... | collective-permute-start | bytes 344072 | tf_op jit(solution)/shard_map/ppermute | solution.py:67
  28.0 10.1 %all-to-all-start = ((bf16[8,2,3584]{2,1,0:T(2,128)(2,1)}), bf16[8,2,3584]{2,1,0:T(2,128)(2,1)S(1)}, u32[]{:S(2)}, u32[]{:S(2)}) async-start(bf16[8,2,3584]{2,1,0:T(2,128)(2,1)} %reshape.58), calls=%async_computation | async-start | bytes 229376 | tf_op jit(solution)/shard_map/all_to_all | solution.py:58
  32.4 69.3 %all-reduce.2.cloned.1.call-start = ((), (), s32[]{:S(2)}) async-start(), calls=%async_computation.3 | async-start | bytes 917504 | tf_op jit(solution)/shard_map/psum | solution.py:104
  32.5 14.8 %collective-permute-start.1 = (bf16[64,1792]{1,0:T(8,128)(2,1)S(1)}, bf16[64,1792]{1,0:T(8,128)(2,1)S(1)}, u32[]{:S(2)}, u32[]{:S(2)}) collective-permute-start(bf16[64,1792]{1,0:T(8,128)(2,1)S(1)} %maximum_select_fusion.1), channel_id=1, source_target_pairs={{0,2},{1,3},{2,0},{3,1},{4,6},{5,7},{6,4},{7,5},{8,10},{9,11},{10,... | collective-permute-start | bytes 688136 | tf_op jit(solution)/shard_map/ppermute | solution.py:67
  39.0 12.3 %copy-start.1 = (bf16[1,640,3584]{2,1,0:T(8,128)(2,1)S(1)}, bf16[1,640,3584]{2,1,0:T(8,128)(2,1)}, u32[]{:S(2)}) copy-start(bf16[1,640,3584]{2,1,0:T(8,128)(2,1)} %param.18) | copy-start | bytes 13762564
  47.3 5.5 %copy-start.2 = (bf16[1,640,3584]{2,1,0:T(8,128)(2,1)S(1)}, bf16[1,640,3584]{2,1,0:T(8,128)(2,1)}, u32[]{:S(2)}) copy-start(bf16[1,640,3584]{2,1,0:T(8,128)(2,1)} %param.19) | copy-start | bytes 13762564
  47.3 7.0 %slice-start = ((s8[4587520]{0:T(1024)(128)(4,1)}), s8[4194304]{0:T(1024)(128)(4,1)S(1)}, s32[]{:S(2)}) async-start(s8[4587520]{0:T(1024)(128)(4,1)} %bitcast.37), calls=%async_computation.4 | async-start | bytes 8388608
  51.3 3.1 %slice-start.1 = ((s8[4587520]{0:T(1024)(128)(4,1)}), s8[393216]{0:T(1024)(128)(4,1)S(1)}, s32[]{:S(2)}) async-start(s8[4587520]{0:T(1024)(128)(4,1)} %bitcast.37), calls=%async_computation.5 | async-start | bytes 786432
  104.7 12.9 %all-to-all-start.2 = ((bf16[8,2,3584]{2,1,0:T(2,128)(2,1)}), bf16[8,2,3584]{2,1,0:T(2,128)(2,1)S(1)}, u32[]{:S(2)}, u32[]{:S(2)}) async-start(bf16[8,2,3584]{2,1,0:T(2,128)(2,1)} %reshape.60), calls=%async_computation.2 | async-start | bytes 229376 | tf_op jit(solution)/shard_map/all_to_all | solution.py:106
Sparse Core Ops, SparseCore 0:
  57.2 44.5 all-reduce.1
